TPU v7x, 256 devices: a whole 4x4x8 slice. The times are simulated.
256 devices in a mesh: row: 16 (over y, x), col: 16 (over z, core).
Axes of the slice: x: 4, y: 4, z: 8, core: 2. Of those that a mesh axis runs over, the one named last changes fastest.
Arguments:
- hidden_in: bfloat16 [1024, 4096], P('col', 'row'), may hold values from -250 to 250
- norm_gain: bfloat16 [4096], P('row'), may hold values from 0.099609375 to 1.8984375
- w_qkv: bfloat16 [4096, 6144], P('row', 'col'), may hold values from -0.125 to 0.125
- w_out: bfloat16 [4096, 4096], P('row', 'col'), may hold values from -0.125 to 0.125
- cache_k: bfloat16 [16, 4096, 1024], P('col', 'row'), may hold values from -1300 to 1300
- value_cache: bfloat16 [16, 4096, 1024], P('col', 'row'), may hold values from -6 to 6
- cache_len: int32 [16], P('col'), may hold values from 1 to 4096, as said below
- parents: int32 [16, 64], P('col'), may hold values from -1 to 62, as said below
Outputs:
- update: bfloat16 [1024, 4096], P('col', 'row')
Inputs may be any that keep to these rules, and one draw needn't show every extreme that they name: Slots 0 to cache_len - 1 of a request's window are filled; some request fills all 4096 slots. `parents`: slot 0 of every request is the root with parent -1; every other slot's parent is an earlier slot of the same request; slot 63 has parent 64 - 2.
All inputs are finite; a program needn't handle non-finite values.
Results may differ from a plain program's by a relative error of at most 0.011.
The roundings to bfloat16 on the way count: a program that leaves them out, or rounds other values in their place, can miss the bound.
Values may be sent and summed in bfloat16 or wider, within the bound.
A program may use at most 128 MiB of HBM per device.

v0:
```python
import jax
import jax.numpy as jnp
from jax import lax
from jax.sharding import PartitionSpec as P

D = 4096
QUERY_HEADS = 32
KEY_VALUE_HEADS = 8
HEAD_SIZE = 128
masked_score = -1e30


def ancestors(parents):
    draft_tree = parents.shape[1]
    slot_ids = jnp.arange(draft_tree, dtype=jnp.int32)
    parent_links = (parents[:, :, None] == slot_ids[None, None, :]).astype(jnp.float32)
    reachable = parent_links + jnp.eye(draft_tree, dtype=jnp.float32)[None]
    for squaring in range(max(1, (draft_tree - 1).bit_length())):
        product = jnp.einsum("rij,rjk->rik", reachable, reachable, precision=lax.Precision.HIGHEST)
        reachable = (product > 0.5).astype(jnp.float32)
    return reachable > 0.5


def row_reduce(partial, axis_name, sent=jnp.float32):
    count = lax.axis_size(axis_name)
    rows, cols = partial.shape
    pieces = partial.reshape(rows, count, cols // count).transpose(1, 0, 2).astype(sent)
    received = lax.all_to_all(pieces, axis_name, 0, 0)
    return jnp.sum(received.astype(jnp.float32), axis=0)


def row_gather(value, axis_name):
    count = lax.axis_size(axis_name)
    copies = jnp.broadcast_to(value[None], (count,) + value.shape)
    return lax.all_to_all(copies, axis_name, 0, 0)


def shards(hidden_in, norm_gain, w_qkv, w_out, cache_k, value_cache, cache_len, parents):
    rows_here = hidden_in.shape[0]
    request_list = cache_k.shape[0]
    token_positions = cache_k.shape[1]
    draft_tree = parents.shape[1]
    head_groups = QUERY_HEADS // KEY_VALUE_HEADS
    row_count = lax.axis_size("row")
    heads_dev = QUERY_HEADS // row_count
    row_index = lax.axis_index("row")
    score_scale = HEAD_SIZE ** (-0.5)
    features = hidden_in.astype(jnp.float32)
    squares = jnp.sum(row_gather(jnp.sum(features * features, axis=1), "row"), axis=0)
    row_scale = lax.rsqrt(squares / D + 1e-05)
    normed = (features * row_scale[:, None] * norm_gain.astype(jnp.float32)[None, :]).astype(
        jnp.bfloat16
    )
    qkv_width = w_qkv.shape[1]
    col_count = lax.axis_size("col")
    feature_rows = w_qkv.shape[0]
    out_rows = -(-w_out.size // qkv_width)
    out_rows = -(-out_rows // 8) * 8
    out_flat = jnp.pad(w_out.reshape(-1), (0, out_rows * qkv_width - w_out.size))
    weights_all = lax.all_gather(
        jnp.concatenate([w_qkv, out_flat.reshape(out_rows, qkv_width)]), "col", axis=1, tiled=True
    )
    weights_all = lax.optimization_barrier(weights_all)
    partial_value = jnp.dot(normed, weights_all[:feature_rows], preferred_element_type=jnp.float32)
    local = (
        jnp.stack([cache_k[0], value_cache[0]])
        .reshape(2, token_positions, KEY_VALUE_HEADS, HEAD_SIZE)
        .transpose(2, 0, 1, 3)
    )
    pieces = jnp.repeat(local, row_count // KEY_VALUE_HEADS, axis=0)
    by_head = lax.all_to_all(pieces, "row", 0, 0)
    by_head, partial_value = lax.optimization_barrier((by_head, partial_value))
    keys = by_head[:, 0].reshape(row_count * token_positions, HEAD_SIZE)
    values = by_head[:, 1].reshape(row_count * token_positions, HEAD_SIZE)
    query_cols = QUERY_HEADS * HEAD_SIZE
    query_part = partial_value[:, :query_cols].reshape(rows_here, row_count, -1)
    pair_part = (
        partial_value[:, query_cols:]
        .reshape(rows_here, 2, KEY_VALUE_HEADS, HEAD_SIZE)
        .transpose(0, 2, 1, 3)
        .reshape(rows_here, row_count, -1)
    )
    owned = jnp.concatenate([query_part, pair_part], axis=2).transpose(1, 0, 2)
    summed = jnp.sum(lax.all_to_all(owned, "row", 0, 0), axis=0).astype(jnp.bfloat16)
    query_mine = summed[:, : heads_dev * HEAD_SIZE]
    pair_mine = summed[:, heads_dev * HEAD_SIZE :]
    partner = [(i, i ^ 1) for i in range(row_count)]
    pair_theirs = lax.ppermute(pair_mine, "row", partner)
    is_key = row_index % 2 == 0
    key_mine = jnp.where(is_key, pair_mine, pair_theirs)
    value_mine = jnp.where(is_key, pair_theirs, pair_mine)
    window = row_count * token_positions
    query_own = query_mine.reshape(draft_tree, heads_dev, HEAD_SIZE)
    scores = (
        jnp.einsum("thd,pd->htp", query_own, keys, preferred_element_type=jnp.float32) * score_scale
    )
    visible = (jnp.arange(window, dtype=jnp.int32) < cache_len[0])[None, None, :]
    scores = jnp.where(visible, scores, masked_score)
    allowed = ancestors(parents)[0][None, :, :]
    tree_scores = (
        jnp.einsum("thd,sd->hts", query_own, key_mine, preferred_element_type=jnp.float32)
        * score_scale
    )
    tree_scores = jnp.where(allowed, tree_scores, masked_score)
    cache_max = jnp.max(scores, axis=-1)
    weights = jnp.where(visible, jnp.exp(scores - cache_max[..., None]), 0.0)
    cache_total = jnp.sum(weights, axis=-1)
    cache_blend = jnp.einsum(
        "htp,pd->htd", weights.astype(jnp.bfloat16), values, preferred_element_type=jnp.float32
    )
    cache_max, cache_total, cache_blend, tree_scores, value_mine = lax.optimization_barrier(
        (cache_max, cache_total, cache_blend, tree_scores, value_mine)
    )
    tree_max = jnp.max(tree_scores, axis=-1)
    tree_weights = jnp.where(allowed, jnp.exp(tree_scores - tree_max[..., None]), 0.0)
    tree_total = jnp.sum(tree_weights, axis=-1)
    tree_blend = jnp.einsum(
        "hts,sd->htd",
        tree_weights.astype(jnp.bfloat16),
        value_mine,
        preferred_element_type=jnp.float32,
    )
    joint_max = jnp.maximum(cache_max, tree_max)
    cache_scale = jnp.exp(cache_max - joint_max)
    tree_scale = jnp.exp(tree_max - joint_max)
    totals = cache_total * cache_scale + tree_total * tree_scale
    blended = cache_blend * cache_scale[..., None] + tree_blend * tree_scale[..., None]
    attended = (blended / totals[..., None]).astype(jnp.bfloat16)
    attended = attended.transpose(1, 0, 2).reshape(rows_here, heads_dev * HEAD_SIZE)
    out_all = (
        weights_all[feature_rows:]
        .reshape(out_rows, col_count, qkv_width)
        .transpose(1, 0, 2)
        .reshape(col_count, -1)[:, : w_out.size]
        .reshape(col_count, w_out.shape[0], w_out.shape[1])
        .transpose(1, 0, 2)
    )
    partial_out = jnp.dot(
        attended, out_all.reshape(w_out.shape[0], -1), preferred_element_type=jnp.float32
    )
    return row_reduce(partial_out, "row", jnp.bfloat16).astype(jnp.bfloat16)


def solution(mesh):
    placed = (
        P("col", "row"),
        P("row"),
        P("row", "col"),
        P("row", "col"),
        P("col", "row", None),
        P("col", "row", None),
        P("col"),
        P("col", None),
    )
    return jax.shard_map(
        shards, mesh=mesh, in_specs=placed, out_specs=P("col", "row"), check_vma=False
    )
```

profile of v0, /device:TPU:2, one launch (start us, length us, event | category | flops | bytes accessed | tf_op | source)
XLA Modules:
  0.0 123.9 jit_solution(737645219438558461)
XLA Ops:
  6.5 0.0 copy-start.2
  6.5 0.0 copy-start.3
  6.5 0.0 all-gather.2.cloned.1.call-start
  6.5 1.1 copy.67
  7.7 0.1 reshape.217
  7.7 1.7 %pad_maximum_fusion.1 = bf16[432,384]{1,0:T(8,128)(2,1)} fusion(bf16[176,384]{1,0:T(8,128)(2,1)S(1)} %reshape.217, bf16[256,384]{1,0:T(8,128)(2,1)} %param.10), kind=kLoop, calls=%fused_computation.34 | loop fusion | flops 663552 | bytes 663552 | tf_op jit(solution)/shard_map/concatenate | solution.py:61
  9.4 0.0 all-gather.2.cloned.1.call-update
  9.4 0.9 fusion.23
  10.3 0.6 broadcast_in_dim.60
  10.9 7.5 %all-to-all-start.1 = ((f32[16,1,64]{2,1,0:T(1,128)}), f32[16,1,64]{2,1,0:T(1,128)S(1)}, u32[]{:S(2)}, u32[]{:S(2)}) async-start(f32[16,1,64]{2,1,0:T(1,128)} %broadcast_in_dim.60), calls=%async_computation.1 | async-start | bytes 16384 | tf_op jit(solution)/shard_map/all_to_all | solution.py:35
  18.4 0.0 copy-done.2
  18.4 0.0 copy-done.3
  18.4 0.1 pad_maximum_fusion
  18.5 0.3 copy.66
  18.8 0.1 bitcast_bitcast_fusion
  18.9 0.2 copy.51
  19.1 5.5 %all-to-all-done.1 = f32[16,1,64]{2,1,0:T(1,128)S(1)} async-done(((f32[16,1,64]{2,1,0:T(1,128)}), f32[16,1,64]{2,1,0:T(1,128)S(1)}, u32[]{:S(2)}, u32[]{:S(2)}) %all-to-all-start.1) | async-done | bytes 4128 | tf_op jit(solution)/shard_map/all_to_all | solution.py:35
  24.6 1.8 %broadcast_in_dim.59 = bf16[8,2,2,256,128]{4,3,2,1,0:T(8,128)(2,1)} broadcast(bf16[8,2,256,128]{3,2,1,0:T(8,128)(2,1)S(1)} %copy.51), dimensions={0,2,3,4} | broadcast | bytes 3145728 | tf_op jit(solution)/shard_map/broadcast_in_dim | solution.py:70
  26.4 5.1 %all-to-all-start = ((bf16[16,2,256,128]{3,2,1,0:T(8,128)(2,1)}), bf16[16,2,256,128]{3,2,1,0:T(8,128)(2,1)S(1)}, u32[]{:S(2)}, u32[]{:S(2)}) async-start(bf16[16,2,256,128]{3,2,1,0:T(8,128)(2,1)} %bitcast.104), calls=%async_computation | async-start | bytes 4194304 | tf_op jit(solution)/shard_map/all_to_all | solution.py:71
  31.5 0.0 copy-done.6
  31.6 25.6 %all-gather.2.cloned.1.call-done = bf16[432,6144]{1,0:T(8,128)(2,1)} async-done(((bf16[432,384]{1,0:T(8,128)(2,1)}), bf16[432,6144]{1,0:T(8,128)(2,1)}) %all-gather.2.cloned.1.call-update) | async-done | bytes 5308432 | tf_op jit(solution)/shard_map/all_gather | solution.py:60
  57.2 0.0 copy-done.4
  57.2 3.8 %fusion.2 = f32[64,6144]{1,0:T(8,128)} fusion(bf16[432,6144]{1,0:T(8,128)(2,1)} %all-gather.2.cloned.1.call-done, bf16[64,256]{1,0:T(8,128)(2,1)S(1)} %copy-done.4, f32[256]{0:T(256)S(1)} %convert_element_type.88, f32[64]{0:T(128)S(1)} %add_rsqrt_fusion), kind=kOutput, calls=%fused_computation.3 | convolution fusion | flops 201392128 | bytes 4752640 | tf_op jit(solution)/shard_map/dot_general | solution.py:64
  61.0 0.0 all-to-all-done
  61.0 1.1 slice_bitcast_fusion
  62.1 0.0 slice-start.1
  62.1 0.1 copy.68
  62.2 0.2 copy.53
  62.4 0.9 slice-done.1
  63.3 0.1 copy.84
  63.5 1.3 %maximum_bitcast_fusion = f32[16,64,384]{2,1,0:T(8,128)} fusion(f32[64,16,128]{2,0,1:T(8,128)S(1)} %bitcast.113, f32[64,16,256]{2,0,1:T(8,128)S(1)} %bitcast.108), kind=kLoop, calls=%fused_computation.11 | loop fusion | flops 393216 | bytes 3145728 | tf_op jit(solution)/shard_map/transpose | solution.py:83
  64.7 7.4 %all-to-all-start.2 = ((f32[16,64,384]{2,1,0:T(8,128)}), f32[16,64,384]{2,1,0:T(8,128)}, u32[]{:S(2)}, u32[]{:S(2)}) async-start(f32[16,64,384]{2,1,0:T(8,128)} %maximum_bitcast_fusion), calls=%async_computation.2 | async-start | bytes 3145728 | tf_op jit(solution)/shard_map/all_to_all | solution.py:84
  72.8 0.0 copy-done.5
  72.8 0.1 fusion.35
  72.9 0.2 convolution_compare_fusion.5
  73.1 0.1 convolution_compare_fusion.4
  73.2 0.1 convolution_compare_fusion.3
  73.4 0.1 convolution_compare_fusion.2
  73.5 0.1 convolution_compare_fusion.1
  73.6 0.1 fusion.17
  73.8 0.1 copy.56
  73.9 0.0 slice-start
  73.9 1.6 %slice-done = bf16[176,6144]{1,0:T(8,128)(2,1)S(1)} async-done(((bf16[432,6144]{1,0:T(8,128)(2,1)}), bf16[176,6144]{1,0:T(8,128)(2,1)S(1)}, s32[]{:S(2)}) %slice-start) | async-done | bytes 2162712 | tf_op jit(solution)/shard_map/slice | solution.py:131
  75.5 0.2 copy.83
  75.8 0.5 copy.69
  76.2 0.1 slice.40
  76.4 1.8 %copy.70 = bf16[2,8,256,256]{3,2,1,0:T(8,128)(2,1)} copy(bf16[2,8,256,256]{3,1,2,0:T(8,128)(2,1)S(1)} %bitcast.105) | data formatting | bytes 4194304
  78.2 3.9 %copy.61 = bf16[256,16,256]{0,2,1:T(8,128)(2,1)} copy(bf16[256,16,256]{2,0,1:T(8,128)(2,1)} %bitcast.106) | data formatting | bytes 4194304 | tf_op jit(solution)/shard_map/transpose | solution.py:136
  82.1 1.2 fusion.56
  83.3 10.9 %all-to-all-done.2 = f32[16,64,384]{2,1,0:T(8,128)} async-done(((f32[16,64,384]{2,1,0:T(8,128)}), f32[16,64,384]{2,1,0:T(8,128)}, u32[]{:S(2)}, u32[]{:S(2)}) %all-to-all-start.2) | async-done | bytes 1572896 | tf_op jit(solution)/shard_map/all_to_all | solution.py:84
  94.1 1.5 %reduce_sum.59 = bf16[64,384]{1,0:T(8,128)(2,1)S(1)} reduce(f32[16,64,384]{2,1,0:T(8,128)} %all-to-all-done.2, f32[]{:T(128)} %constant.12.clone.1), dimensions={0}, to_apply=%region_2.3 | reduce | flops 368640 | bytes 1622020 | tf_op jit(solution)/shard_map/reduce_sum | solution.py:84
  95.6 3.6 %collective-permute-start = (bf16[64,128]{1,0:T(8,128)(2,1)S(1)}, bf16[64,128]{1,0:T(8,128)(2,1)S(1)}, u32[]{:S(2)}, u32[]{:S(2)}) collective-permute-start(bf16[64,128]{1,0:T(8,128)(2,1)S(1)} %slice.38), channel_id=1, source_target_pairs={{0,16},{16,0},{32,48},{48,32},{64,80},{80,64},{96,112},{112,96},{1... | collective-permute-start | bytes 49160 | tf_op jit(solution)/shard_map/ppermute | solution.py:88
  99.3 0.5 fusion.57
  99.8 0.0 copy-done.1
  99.8 0.5 fusion.18
  100.3 0.0 copy-start
  100.4 0.5 fusion.7
  100.9 0.1 collective-permute-done
  101.0 0.2 fusion.15
  101.3 0.2 fusion.31
  101.5 0.4 copy-done
  101.9 0.8 fusion.11
  102.7 13.7 %all_to_all.21 = bf16[16,64,256]{2,1,0:T(8,128)(2,1)S(1)} all-to-all(bf16[16,64,256]{2,1,0:T(8,128)(2,1)S(1)} %fusion.11), channel_id=1, replica_groups=mesh['row'=16,'col'=16] {'row'}, dimensions={0} | all-to-all | bytes 1048576 | tf_op jit(solution)/shard_map/all_to_all | solution.py:28
  116.3 0.7 reduce_sum.62
  (16 shorter events, 0.2 us)
Async XLA Ops:
  6.5 11.9 %copy-start.2 = (bf16[1,256,1024]{2,1,0:T(8,128)(2,1)S(1)}, bf16[1,256,1024]{2,1,0:T(8,128)(2,1)}, u32[]{:S(2)}) copy-start(bf16[1,256,1024]{2,1,0:T(8,128)(2,1)} %param.13) | copy-start | bytes 1572868
  6.5 11.9 %copy-start.3 = (bf16[1,256,1024]{2,1,0:T(8,128)(2,1)S(1)}, bf16[1,256,1024]{2,1,0:T(8,128)(2,1)}, u32[]{:S(2)}) copy-start(bf16[1,256,1024]{2,1,0:T(8,128)(2,1)} %param.12) | copy-start | bytes 1572868
  6.5 50.6 %all-gather.2.cloned.1.call-start = ((), (), s32[]{:S(2)}) async-start(), calls=%async_computation.4 | async-start | bytes 5640192 | tf_op jit(solution)/shard_map/all_gather | solution.py:60
  10.9 13.6 %all-to-all-start.1 = ((f32[16,1,64]{2,1,0:T(1,128)}), f32[16,1,64]{2,1,0:T(1,128)S(1)}, u32[]{:S(2)}, u32[]{:S(2)}) async-start(f32[16,1,64]{2,1,0:T(1,128)} %broadcast_in_dim.60), calls=%async_computation.1 | async-start | bytes 16384 | tf_op jit(solution)/shard_map/all_to_all | solution.py:35
  26.4 5.1 %copy-start.6 = (bf16[256]{0:T(256)(128)(2,1)S(1)}, bf16[256]{0:T(256)(128)(2,1)}, u32[]{:S(2)}) copy-start(bf16[256]{0:T(256)(128)(2,1)} %param.9) | copy-start | bytes 1540
  26.4 30.8 %copy-start.4 = (bf16[64,256]{1,0:T(8,128)(2,1)S(1)}, bf16[64,256]{1,0:T(8,128)(2,1)}, u32[]{:S(2)}) copy-start(bf16[64,256]{1,0:T(8,128)(2,1)} %param.8) | copy-start | bytes 98308
  26.4 34.6 %all-to-all-start = ((bf16[16,2,256,128]{3,2,1,0:T(8,128)(2,1)}), bf16[16,2,256,128]{3,2,1,0:T(8,128)(2,1)S(1)}, u32[]{:S(2)}, u32[]{:S(2)}) async-start(bf16[16,2,256,128]{3,2,1,0:T(8,128)(2,1)} %bitcast.104), calls=%async_computation | async-start | bytes 4194304 | tf_op jit(solution)/shard_map/all_to_all | solution.py:71
  62.1 1.2 slice-start.1
  64.7 8.1 %copy-start.5 = (s32[1,64]{1,0:T(1,128)S(1)}, s32[1,64]{1,0:T(1,128)}, u32[]{:S(2)}) copy-start(s32[1,64]{1,0:T(1,128)} %param.15) | copy-start | bytes 772
  64.7 29.4 %all-to-all-start.2 = ((f32[16,64,384]{2,1,0:T(8,128)}), f32[16,64,384]{2,1,0:T(8,128)}, u32[]{:S(2)}, u32[]{:S(2)}) async-start(f32[16,64,384]{2,1,0:T(8,128)} %maximum_bitcast_fusion), calls=%async_computation.2 | async-start | bytes 3145728 | tf_op jit(solution)/shard_map/all_to_all | solution.py:84
  73.9 1.6 %slice-start = ((bf16[432,6144]{1,0:T(8,128)(2,1)}), bf16[176,6144]{1,0:T(8,128)(2,1)S(1)}, s32[]{:S(2)}) async-start(bf16[432,6144]{1,0:T(8,128)(2,1)} %all-gather.2.cloned.1.call-done), calls=%async_computation.5 | async-start | bytes 4325376 | tf_op jit(solution)/shard_map/slice | solution.py:131
  83.3 16.5 %copy-start.1 = (bf16[16,1,256,128]{3,2,1,0:T(8,128)(2,1)S(1)}, bf16[16,1,256,128]{3,2,1,0:T(8,128)(2,1)}, u32[]{:S(2)}) copy-start(bf16[16,1,256,128]{3,2,1,0:T(8,128)(2,1)} %get-tuple-element.22) | copy-start | bytes 3145732
  95.6 5.3 %collective-permute-start = (bf16[64,128]{1,0:T(8,128)(2,1)S(1)}, bf16[64,128]{1,0:T(8,128)(2,1)S(1)}, u32[]{:S(2)}, u32[]{:S(2)}) collective-permute-start(bf16[64,128]{1,0:T(8,128)(2,1)S(1)} %slice.38), channel_id=1, source_target_pairs={{0,16},{16,0},{32,48},{48,32},{64,80},{80,64},{96,112},{112,96},{1... | collective-permute-start | bytes 49160 | tf_op jit(solution)/shard_map/ppermute | solution.py:88
  100.3 1.6 %copy-start = (bf16[256,16,256]{0,2,1:T(8,128)(2,1)S(1)}, bf16[256,16,256]{0,2,1:T(8,128)(2,1)}, u32[]{:S(2)}) copy-start(bf16[256,16,256]{0,2,1:T(8,128)(2,1)} %copy.61) | copy-start | bytes 6291460
Sparse Core Ops, SparseCore 0:
  9.6 47.5 all-gather.1
where the time goes:
time: 125 us; the launch traced here: 124 us
  waiting for transfers between devices  42.1 us (34%)
  starting transfers between devices  23.6 us (19%)
  local copies, waits for them, and re-layouts  16.5 us (13%)
  between operations  14.3 us (11%)
  blocking collectives  13.7 us (11%)
  other arithmetic  6.9 us (6%)
  matrix products  6.86 us (5%)
    all_gather x1, waiting for transfers between devices, shards(): lax.all_gather(jnp.concatenate([w_qkv, out_flat.reshape(out_rows, qkv_wid...  25.6 us
    all_to_all x1, blocking collectives, row_reduce(): received = lax.all_to_all(pieces, axis_name, 0, 0)  13.7 us
    all_to_all x1, waiting for transfers between devices, shards(): lax.all_to_all(owned, 'row', 0, 0)  10.9 us
    all_to_all x1, starting transfers between devices, row_gather(): return lax.all_to_all(copies, axis_name, 0, 0)  7.48 us
    all_to_all x1, starting transfers between devices, shards(): lax.all_to_all(owned, 'row', 0, 0)  7.4 us
    all_to_all x1, waiting for transfers between devices, row_gather(): return lax.all_to_all(copies, axis_name, 0, 0)  5.47 us
    unnamed x20, local copies, waits for them, and re-layouts  5.21 us
    all_to_all x1, starting transfers between devices, shards(): by_head = lax.all_to_all(pieces, 'row', 0, 0)  5.13 us
  transfers between devices with their start and end apart: 5, of which 4 were waited for; matrix products, arithmetic and copies ran while one was open for 15% of the time, Pallas kernels for 0%

commit v1 on v0

--- a/solution.py
+++ b/solution.py
@@ -8,6 +8,12 @@
 KEY_VALUE_HEADS = 8
 HEAD_SIZE = 128
 masked_score = -1e30
+
+
+def in_order(blocks, dim):
+    blocks = jnp.moveaxis(blocks, 0, dim)
+    shape = blocks.shape
+    return blocks.reshape(*shape[:dim], shape[dim] * shape[dim + 1], *shape[dim + 2 :])
 
 
 def ancestors(parents):
@@ -57,9 +63,20 @@
     out_rows = -(-w_out.size // qkv_width)
     out_rows = -(-out_rows // 8) * 8
     out_flat = jnp.pad(w_out.reshape(-1), (0, out_rows * qkv_width - w_out.size))
-    weights_all = lax.all_gather(
-        jnp.concatenate([w_qkv, out_flat.reshape(out_rows, qkv_width)]), "col", axis=1, tiled=True
-    )
+    shard = jnp.concatenate([w_qkv, out_flat.reshape(out_rows, qkv_width)])
+    count_2 = lax.axis_size("col")
+    pairs = [(i_2, (i_2 + 1) % count_2) for i_2 in range(count_2)]
+    back = [(b, a) for a, b in pairs]
+    lower, upper = ([], [])
+    for step in range(count_2 - 1):
+        if step % 2 == 0:
+            lower.append(lax.ppermute(lower[-1] if lower else shard, "col", pairs))
+        else:
+            upper.append(lax.ppermute(upper[-1] if upper else shard, "col", back))
+    tiles = jnp.stack([*lower[::-1], shard, *upper])
+    shift = lax.axis_index("col") - len(lower)
+    tiles = tiles[(jnp.arange(count_2) - shift) % count_2]
+    weights_all = in_order(tiles, 1)
     weights_all = lax.optimization_barrier(weights_all)
     partial_value = jnp.dot(normed, weights_all[:feature_rows], preferred_element_type=jnp.float32)
     local = (

time: 125 us -> 165 us (1.32); the launches traced: 124 us -> 162 us
  local copies, waits for them, and re-layouts: 16.5 us -> 50.2 us
  starting transfers between devices: 23.6 us -> 44 us
  between operations: 14.3 us -> 1.07 us
    ppermute x0 -> x15, waiting for transfers between devices: none -> 32.6 us  [the longest x8 27.8 us: shards(): lower.append(lax.ppermute(lower[-1] if lower else shard, 'col', pairs))]
    all_gather x1 -> x0, waiting for transfers between devices: 25.6 us -> none  [shards(): lax.all_gather(jnp.concatenate([w_qkv, out_flat.reshape(out_rows, qkv_wid...]
    unnamed x20 -> x52, local copies, waits for them, and re-layouts: 5.21 us -> 28 us
    ppermute x0 -> x15, starting transfers between devices: none -> 20 us  [the longest x7 19.9 us: shards(): upper.append(lax.ppermute(upper[-1] if upper else shard, 'col', back))]
    gather x0 -> x1, local copies, waits for them, and re-layouts: none -> 6.2 us  [shards(): tiles = tiles[(jnp.arange(count_2) - shift) % count_2]]
    all_to_all x1, waiting for transfers between devices: 5.47 us -> 0.01 us  [row_gather(): return lax.all_to_all(copies, axis_name, 0, 0)]
    reshape x1 -> x2, local copies, waits for them, and re-layouts: 0.07 us -> 3.54 us  [the longest x1 3.47 us: in_order(): blocks.reshape(*shape[:dim], shape[dim] * shape[dim + 1], *shape[dim + 2:])]
    all_to_all x1, waiting for transfers between devices: 10.9 us -> 8.75 us  [shards(): lax.all_to_all(owned, 'row', 0, 0)]
  transfers between devices with their start and end apart: 5 -> 19, of which waited for: 4 -> 8; matrix products, arithmetic and copies ran while one was open for 15% -> 31% of each run, Pallas kernels for 0% -> 0%
where the time goes in v1:
time: 165 us; the launch traced here: 162 us
  local copies, waits for them, and re-layouts  50.2 us (30%)
  starting transfers between devices  44 us (27%)
  waiting for transfers between devices  41.4 us (25%)
  blocking collectives  12.9 us (8%)
  other arithmetic  6.5 us (4%)
  matrix products  6.12 us (4%)
    unnamed x52, local copies, waits for them, and re-layouts  28 us
    ppermute x8, waiting for transfers between devices, shards(): lower.append(lax.ppermute(lower[-1] if lower else shard, 'col', pairs))  27.8 us
    ppermute x7, starting transfers between devices, shards(): upper.append(lax.ppermute(upper[-1] if upper else shard, 'col', back))  19.9 us
    all_to_all x1, blocking collectives, row_reduce(): received = lax.all_to_all(pieces, axis_name, 0, 0)  12.9 us
    all_to_all x1, waiting for transfers between devices, shards(): lax.all_to_all(owned, 'row', 0, 0)  8.75 us
    all_to_all x1, starting transfers between devices, row_gather(): return lax.all_to_all(copies, axis_name, 0, 0)  7.48 us
    all_to_all x1, starting transfers between devices, shards(): by_head = lax.all_to_all(pieces, 'row', 0, 0)  7.23 us
    all_to_all x1, starting transfers between devices, shards(): lax.all_to_all(owned, 'row', 0, 0)  7.23 us
  transfers between devices with their start and end apart: 19, of which 8 were waited for; matrix products, arithmetic and copies ran while one was open for 31% of the time, Pallas kernels for 0%

profile of v1, /device:TPU:2, one launch (start us, length us, event | category | flops | bytes accessed | tf_op | source)
XLA Modules:
  0.0 162.2 jit_solution(6754609644260264497)
XLA Ops:
  0.0 1.0 copy.73
  1.1 0.9 constant_dynamic-update-slice_fusion.1
  2.1 10.1 %collective-permute-done = bf16[432,384]{1,0:T(8,128)(2,1)S(1)} collective-permute-done((bf16[432,384]{1,0:T(8,128)(2,1)S(1)}, bf16[432,384]{1,0:T(8,128)(2,1)S(1)}, u32[]{:S(2)}, u32[]{:S(2)}) %collective-permute-start) | collective-permute-done | bytes 331808 | tf_op jit(solution)/shard_map/ppermute | solution.py:73
  12.2 3.0 %collective-permute-start.8 = (bf16[432,384]{1,0:T(8,128)(2,1)S(1)}, bf16[432,384]{1,0:T(8,128)(2,1)S(1)}, u32[]{:S(2)}, u32[]{:S(2)}) collective-permute-start(bf16[432,384]{1,0:T(8,128)(2,1)S(1)} %constant_dynamic-update-slice_fusion), channel_id=1, source_target_pairs={{1,0},{2,1},{3,2},{4,3},{5,4},{6,5},{7,6},{8,7},{9,8},{10,9},{11,1... | collective-permute-start | bytes 995336 | tf_op jit(solution)/shard_map/ppermute | solution.py:75
  15.2 4.8 %collective-permute-done.1 = bf16[432,384]{1,0:T(8,128)(2,1)S(1)} collective-permute-done((bf16[432,384]{1,0:T(8,128)(2,1)S(1)}, bf16[432,384]{1,0:T(8,128)(2,1)S(1)}, u32[]{:S(2)}, u32[]{:S(2)}) %collective-permute-start.1) | collective-permute-done | bytes 331808 | tf_op jit(solution)/shard_map/ppermute | solution.py:73
  20.0 3.0 %collective-permute-start.9 = (bf16[432,384]{1,0:T(8,128)(2,1)S(1)}, bf16[432,384]{1,0:T(8,128)(2,1)S(1)}, u32[]{:S(2)}, u32[]{:S(2)}) collective-permute-start(bf16[432,384]{1,0:T(8,128)(2,1)S(1)} %collective-permute-done.8), channel_id=1, source_target_pairs={{1,0},{2,1},{3,2},{4,3},{5,4},{6,5},{7,6},{8,7},{9,8},{10,9},{11,1... | collective-permute-start | bytes 995336 | tf_op jit(solution)/shard_map/ppermute | solution.py:75
  22.9 4.8 %collective-permute-done.2 = bf16[432,384]{1,0:T(8,128)(2,1)S(1)} collective-permute-done((bf16[432,384]{1,0:T(8,128)(2,1)S(1)}, bf16[432,384]{1,0:T(8,128)(2,1)S(1)}, u32[]{:S(2)}, u32[]{:S(2)}) %collective-permute-start.2) | collective-permute-done | bytes 331808 | tf_op jit(solution)/shard_map/ppermute | solution.py:73
  27.7 0.8 copy-done.2
  28.5 2.9 %collective-permute-start.10 = (bf16[432,384]{1,0:T(8,128)(2,1)S(1)}, bf16[432,384]{1,0:T(8,128)(2,1)S(1)}, u32[]{:S(2)}, u32[]{:S(2)}) collective-permute-start(bf16[432,384]{1,0:T(8,128)(2,1)S(1)} %collective-permute-done.9), channel_id=1, source_target_pairs={{1,0},{2,1},{3,2},{4,3},{5,4},{6,5},{7,6},{8,7},{9,8},{10,9},{11,1... | collective-permute-start | bytes 995336 | tf_op jit(solution)/shard_map/ppermute | solution.py:75
  31.4 4.1 %collective-permute-done.3 = bf16[432,384]{1,0:T(8,128)(2,1)S(1)} collective-permute-done((bf16[432,384]{1,0:T(8,128)(2,1)S(1)}, bf16[432,384]{1,0:T(8,128)(2,1)S(1)}, u32[]{:S(2)}, u32[]{:S(2)}) %collective-permute-start.3) | collective-permute-done | bytes 331808 | tf_op jit(solution)/shard_map/ppermute | solution.py:73
  35.5 0.6 collective-permute-done.10
  36.1 3.1 %collective-permute-start.11 = (bf16[432,384]{1,0:T(8,128)(2,1)S(1)}, bf16[432,384]{1,0:T(8,128)(2,1)S(1)}, u32[]{:S(2)}, u32[]{:S(2)}) collective-permute-start(bf16[432,384]{1,0:T(8,128)(2,1)S(1)} %collective-permute-done.10), channel_id=1, source_target_pairs={{1,0},{2,1},{3,2},{4,3},{5,4},{6,5},{7,6},{8,7},{9,8},{10,9},{11,1... | collective-permute-start | bytes 995336 | tf_op jit(solution)/shard_map/ppermute | solution.py:75
  39.2 4.1 %collective-permute-done.4 = bf16[432,384]{1,0:T(8,128)(2,1)S(1)} collective-permute-done((bf16[432,384]{1,0:T(8,128)(2,1)S(1)}, bf16[432,384]{1,0:T(8,128)(2,1)S(1)}, u32[]{:S(2)}, u32[]{:S(2)}) %collective-permute-start.4) | collective-permute-done | bytes 331808 | tf_op jit(solution)/shard_map/ppermute | solution.py:73
  43.2 0.9 fusion.23
  44.1 0.6 broadcast_in_dim.61
  44.8 7.5 %all-to-all-start.1 = ((f32[16,1,64]{2,1,0:T(1,128)}), f32[16,1,64]{2,1,0:T(1,128)S(1)}, u32[]{:S(2)}, u32[]{:S(2)}) async-start(f32[16,1,64]{2,1,0:T(1,128)} %broadcast_in_dim.61), calls=%async_computation.1 | async-start | bytes 16384 | tf_op jit(solution)/shard_map/all_to_all | solution.py:41
  52.2 1.3 pad_maximum_fusion
  53.6 2.4 %collective-permute-start.12 = (bf16[432,384]{1,0:T(8,128)(2,1)S(1)}, bf16[432,384]{1,0:T(8,128)(2,1)}, u32[]{:S(2)}, u32[]{:S(2)}) collective-permute-start(bf16[432,384]{1,0:T(8,128)(2,1)S(1)} %collective-permute-done.11), channel_id=1, source_target_pairs={{1,0},{2,1},{3,2},{4,3},{5,4},{6,5},{7,6},{8,7},{9,8},{10,9},{11,1... | collective-permute-start | bytes 995336 | tf_op jit(solution)/shard_map/ppermute | solution.py:75
  56.0 0.3 copy.72
  56.3 4.3 %collective-permute-done.12 = bf16[432,384]{1,0:T(8,128)(2,1)} collective-permute-done((bf16[432,384]{1,0:T(8,128)(2,1)S(1)}, bf16[432,384]{1,0:T(8,128)(2,1)}, u32[]{:S(2)}, u32[]{:S(2)}) %collective-permute-start.12) | collective-permute-done | bytes 331808 | tf_op jit(solution)/shard_map/ppermute | solution.py:75
  60.6 3.2 %collective-permute-start.13 = (bf16[432,384]{1,0:T(8,128)(2,1)}, bf16[432,384]{1,0:T(8,128)(2,1)}, u32[]{:S(2)}, u32[]{:S(2)}) collective-permute-start(bf16[432,384]{1,0:T(8,128)(2,1)} %collective-permute-done.12), channel_id=1, source_target_pairs={{1,0},{2,1},{3,2},{4,3},{5,4},{6,5},{7,6},{8,7},{9,8},{10,9},{11,1... | collective-permute-start | bytes 995336 | tf_op jit(solution)/shard_map/ppermute | solution.py:75
  63.9 0.2 copy.55
  64.1 1.8 %broadcast_in_dim.60 = bf16[8,2,2,256,128]{4,3,2,1,0:T(8,128)(2,1)} broadcast(bf16[8,2,256,128]{3,2,1,0:T(8,128)(2,1)S(1)} %copy.55), dimensions={0,2,3,4} | broadcast | bytes 3145728 | tf_op jit(solution)/shard_map/broadcast_in_dim | solution.py:87
  65.9 7.2 %all-to-all-start = ((bf16[16,2,256,128]{3,2,1,0:T(8,128)(2,1)}), bf16[16,2,256,128]{3,2,1,0:T(8,128)(2,1)S(1)}, u32[]{:S(2)}, u32[]{:S(2)}) async-start(bf16[16,2,256,128]{3,2,1,0:T(8,128)(2,1)} %bitcast.144), calls=%async_computation | async-start | bytes 4194304 | tf_op jit(solution)/shard_map/all_to_all | solution.py:88
  73.2 2.4 %collective-permute-start.14 = (bf16[432,384]{1,0:T(8,128)(2,1)}, bf16[432,384]{1,0:T(8,128)(2,1)S(1)}, u32[]{:S(2)}, u32[]{:S(2)}) collective-permute-start(bf16[432,384]{1,0:T(8,128)(2,1)} %collective-permute-done.13), channel_id=1, source_target_pairs={{1,0},{2,1},{3,2},{4,3},{5,4},{6,5},{7,6},{8,7},{9,8},{10,9},{11,1... | collective-permute-start | bytes 995336 | tf_op jit(solution)/shard_map/ppermute | solution.py:75
  75.6 1.7 %bitcast_dynamic-update-slice_fusion.15 = bf16[16,432,384]{2,1,0:T(8,128)(2,1)} fusion(bf16[432,384]{1,0:T(8,128)(2,1)} %collective-permute-done.7), kind=kLoop, calls=%fused_computation.50 | loop fusion | bytes 663552
  77.3 1.7 %bitcast_dynamic-update-slice_fusion.14 = bf16[16,432,384]{2,1,0:T(8,128)(2,1)} fusion(bf16[16,432,384]{2,1,0:T(8,128)(2,1)} %bitcast_dynamic-update-slice_fusion.15, bf16[432,384]{1,0:T(8,128)(2,1)} %collective-permute-done.6), kind=kLoop, calls=%fused_computation.49 | loop fusion | bytes 663552
  79.1 1.7 %bitcast_dynamic-update-slice_fusion.13 = bf16[16,432,384]{2,1,0:T(8,128)(2,1)} fusion(bf16[16,432,384]{2,1,0:T(8,128)(2,1)} %bitcast_dynamic-update-slice_fusion.14, bf16[432,384]{1,0:T(8,128)(2,1)} %copy-done.11), kind=kLoop, calls=%fused_computation.48 | loop fusion | bytes 663552
  80.8 1.7 %bitcast_dynamic-update-slice_fusion.12 = bf16[16,432,384]{2,1,0:T(8,128)(2,1)} fusion(bf16[16,432,384]{2,1,0:T(8,128)(2,1)} %bitcast_dynamic-update-slice_fusion.13, bf16[432,384]{1,0:T(8,128)(2,1)} %copy-done.10), kind=kLoop, calls=%fused_computation.47 | loop fusion | bytes 663552
  82.6 1.7 %bitcast_dynamic-update-slice_fusion.11 = bf16[16,432,384]{2,1,0:T(8,128)(2,1)} fusion(bf16[16,432,384]{2,1,0:T(8,128)(2,1)} %bitcast_dynamic-update-slice_fusion.12, bf16[432,384]{1,0:T(8,128)(2,1)} %copy-done.9), kind=kLoop, calls=%fused_computation.46 | loop fusion | bytes 663552
  84.3 1.7 %bitcast_dynamic-update-slice_fusion.10 = bf16[16,432,384]{2,1,0:T(8,128)(2,1)} fusion(bf16[16,432,384]{2,1,0:T(8,128)(2,1)} %bitcast_dynamic-update-slice_fusion.11, bf16[432,384]{1,0:T(8,128)(2,1)} %copy-done.4), kind=kLoop, calls=%fused_computation.45 | loop fusion | bytes 663552
  86.0 0.8 bitcast_dynamic-update-slice_fusion.9
  86.8 0.8 bitcast_dynamic-update-slice_fusion.8
  87.6 0.8 bitcast_dynamic-update-slice_fusion.7
  88.3 0.8 bitcast_dynamic-update-slice_fusion.6
  89.1 0.8 bitcast_dynamic-update-slice_fusion.5
  89.8 0.8 bitcast_dynamic-update-slice_fusion.4
  90.6 0.8 bitcast_dynamic-update-slice_fusion.3
  91.4 1.7 %bitcast_dynamic-update-slice_fusion.2 = bf16[16,432,384]{2,1,0:T(8,128)(2,1)} fusion(bf16[16,432,384]{2,1,0:T(8,128)(2,1)} %bitcast_dynamic-update-slice_fusion.3, bf16[432,384]{1,0:T(8,128)(2,1)} %collective-permute-done.12), kind=kLoop, calls=%fused_computation.37 | loop fusion | bytes 663552
  93.1 1.7 %bitcast_dynamic-update-slice_fusion.1 = bf16[16,432,384]{2,1,0:T(8,128)(2,1)} fusion(bf16[16,432,384]{2,1,0:T(8,128)(2,1)} %bitcast_dynamic-update-slice_fusion.2, bf16[432,384]{1,0:T(8,128)(2,1)} %collective-permute-done.13), kind=kLoop, calls=%fused_computation.36 | loop fusion | bytes 663552
  94.8 0.8 bitcast_dynamic-update-slice_fusion
  95.6 6.2 %gather_fusion = bf16[16,432,384]{2,1,0:T(8,128)(2,1)} fusion(bf16[16,432,384]{2,1,0:T(8,128)(2,1)} %bitcast_dynamic-update-slice_fusion, s32[1024]{0:T(1024)S(1)} %pad_clamp_fusion), kind=kCustom, calls=%fused_computation | custom fusion | bytes 10616896 | tf_op jit(solution)/shard_map/gather | solution.py:78
  101.8 3.5 %copy.71 = bf16[16,54,8,384]{3,2,0,1:T(8,128)(2,1)S(1)} copy(bf16[16,54,8,384]{3,2,1,0:T(8,128)(2,1)} %bitcast.140) | data formatting | bytes 10616832 | tf_op jit(solution)/shard_map/reshape | solution.py:16
  105.3 2.3 %copy-done = bf16[16,54,8,384]{3,2,0,1:T(8,128)(2,1)} copy-done((bf16[16,54,8,384]{3,2,0,1:T(8,128)(2,1)}, bf16[16,54,8,384]{3,2,0,1:T(8,128)(2,1)S(1)}, u32[]{:S(2)}) %copy-start) | copy-done | bytes 5308440
  107.6 1.9 %fusion.2 = f32[64,6144]{1,0:T(8,128)} fusion(bf16[432,6144]{1,0:T(8,128)(2,1)S(1)} %bitcast.138, bf16[64,256]{1,0:T(8,128)(2,1)S(1)} %copy-done.12, f32[256]{0:T(256)S(1)} %convert_element_type.88, f32[64]{0:T(128)S(1)} %add_rsqrt_fusion), kind=kOutput, calls=%fused_computation.4 | convolution fusion | flops 201392128 | bytes 4752896 | tf_op jit(solution)/shard_map/dot_general | solution.py:81
  109.5 1.3 slice.29
  110.8 1.1 slice_bitcast_fusion
  112.3 1.3 maximum_bitcast_fusion
  113.6 7.2 %all-to-all-start.2 = ((f32[16,64,384]{2,1,0:T(8,128)}), f32[16,64,384]{2,1,0:T(8,128)}, u32[]{:S(2)}, u32[]{:S(2)}) async-start(f32[16,64,384]{2,1,0:T(8,128)} %maximum_bitcast_fusion), calls=%async_computation.2 | async-start | bytes 3145728 | tf_op jit(solution)/shard_map/all_to_all | solution.py:101
  122.6 1.8 %slice.41 = bf16[176,6144]{1,0:T(8,128)(2,1)S(1)} slice(bf16[432,6144]{1,0:T(8,128)(2,1)} %bitcast.139), slice={[256:432], [0:6144]} | slice | bytes 4325376 | tf_op jit(solution)/shard_map/slice | solution.py:148
  124.4 0.2 copy.89
  124.6 0.5 copy.75
  125.2 1.8 %copy.76 = bf16[2,8,256,256]{3,2,1,0:T(8,128)(2,1)} copy(bf16[2,8,256,256]{3,1,2,0:T(8,128)(2,1)S(1)} %bitcast.145) | data formatting | bytes 4194304
  127.0 3.9 %copy.66 = bf16[256,16,256]{0,2,1:T(8,128)(2,1)} copy(bf16[256,16,256]{2,0,1:T(8,128)(2,1)} %bitcast.146) | data formatting | bytes 4194304 | tf_op jit(solution)/shard_map/transpose | solution.py:153
  131.0 1.2 fusion.58
  132.1 8.7 %all-to-all-done.2 = f32[16,64,384]{2,1,0:T(8,128)} async-done(((f32[16,64,384]{2,1,0:T(8,128)}), f32[16,64,384]{2,1,0:T(8,128)}, u32[]{:S(2)}, u32[]{:S(2)}) %all-to-all-start.2) | async-done | bytes 1572896 | tf_op jit(solution)/shard_map/all_to_all | solution.py:101
  140.9 1.5 reduce_sum.59
  142.4 2.1 %collective-permute-start.15 = (bf16[64,128]{1,0:T(8,128)(2,1)S(1)}, bf16[64,128]{1,0:T(8,128)(2,1)S(1)}, u32[]{:S(2)}, u32[]{:S(2)}) collective-permute-start(bf16[64,128]{1,0:T(8,128)(2,1)S(1)} %slice.40), channel_id=1, source_target_pairs={{0,16},{16,0},{32,48},{48,32},{64,80},{80,64},{96,112},{112,96},{1... | collective-permute-start | bytes 49160 | tf_op jit(solution)/shard_map/ppermute | solution.py:105
  144.4 0.5 fusion.59
  145.0 1.8 %fusion.18 = f32[2,64,128]{2,1,0:T(8,128)S(1)} fusion(bf16[4096,128,1]{1,0,2:T(8,128)(2,1)} %bitcast.154, f32[2,64,4096]{2,1,0:T(8,128)S(1)} %get-tuple-element.25, f32[2,64]{1,0:T(2,128)S(1)} %get-tuple-element.15, pred[4096]{0:T(1024)(128)(4,1)S(1)} %iota_compare_fusion), kind=kOutput, calls=%fused_computation.27 | convolution fusion | flops 135790592 | bytes 3215872 | tf_op jit(solution)/shard_map/htp,pd->htd/dot_general | solution.py:125
  146.7 0.5 fusion.7
  147.8 0.8 fusion.11
  148.6 12.9 %all_to_all.21 = bf16[16,64,256]{2,1,0:T(8,128)(2,1)S(1)} all-to-all(bf16[16,64,256]{2,1,0:T(8,128)(2,1)S(1)} %fusion.11), channel_id=1, replica_groups=mesh['row'=16,'col'=16] {'row'}, dimensions={0} | all-to-all | bytes 1048576 | tf_op jit(solution)/shard_map/all_to_all | solution.py:34
  161.5 0.7 reduce_sum.62
  (78 shorter events, 2.5 us)
Async XLA Ops:
  0.0 63.9 %copy-start.14 = (bf16[256]{0:T(256)(128)(2,1)S(1)}, bf16[256]{0:T(256)(128)(2,1)}, u32[]{:S(2)}) copy-start(bf16[256]{0:T(256)(128)(2,1)} %param.9) | copy-start | bytes 1540
  2.1 10.1 %collective-permute-start = (bf16[432,384]{1,0:T(8,128)(2,1)S(1)}, bf16[432,384]{1,0:T(8,128)(2,1)S(1)}, u32[]{:S(2)}, u32[]{:S(2)}) collective-permute-start(bf16[432,384]{1,0:T(8,128)(2,1)S(1)} %constant_dynamic-update-slice_fusion), channel_id=1, source_target_pairs={{0,1},{1,2},{2,3},{3,4},{4,5},{5,6},{6,7},{7,8},{8,9},{9,10},{10,1... | collective-permute-start | bytes 995336 | tf_op jit(solution)/shard_map/ppermute | solution.py:73
  12.2 7.8 %collective-permute-start.1 = (bf16[432,384]{1,0:T(8,128)(2,1)S(1)}, bf16[432,384]{1,0:T(8,128)(2,1)S(1)}, u32[]{:S(2)}, u32[]{:S(2)}) collective-permute-start(bf16[432,384]{1,0:T(8,128)(2,1)S(1)} %collective-permute-done), channel_id=1, source_target_pairs={{0,1},{1,2},{2,3},{3,4},{4,5},{5,6},{6,7},{7,8},{8,9},{9,10},{10,1... | collective-permute-start | bytes 995336 | tf_op jit(solution)/shard_map/ppermute | solution.py:73
  12.2 7.8 %collective-permute-start.8 = (bf16[432,384]{1,0:T(8,128)(2,1)S(1)}, bf16[432,384]{1,0:T(8,128)(2,1)S(1)}, u32[]{:S(2)}, u32[]{:S(2)}) collective-permute-start(bf16[432,384]{1,0:T(8,128)(2,1)S(1)} %constant_dynamic-update-slice_fusion), channel_id=1, source_target_pairs={{1,0},{2,1},{3,2},{4,3},{5,4},{6,5},{7,6},{8,7},{9,8},{10,9},{11,1... | collective-permute-start | bytes 995336 | tf_op jit(solution)/shard_map/ppermute | solution.py:75
  20.0 7.8 %collective-permute-start.2 = (bf16[432,384]{1,0:T(8,128)(2,1)S(1)}, bf16[432,384]{1,0:T(8,128)(2,1)S(1)}, u32[]{:S(2)}, u32[]{:S(2)}) collective-permute-start(bf16[432,384]{1,0:T(8,128)(2,1)S(1)} %collective-permute-done.1), channel_id=1, source_target_pairs={{0,1},{1,2},{2,3},{3,4},{4,5},{5,6},{6,7},{7,8},{8,9},{9,10},{10,1... | collective-permute-start | bytes 995336 | tf_op jit(solution)/shard_map/ppermute | solution.py:73
  20.0 7.8 %collective-permute-start.9 = (bf16[432,384]{1,0:T(8,128)(2,1)S(1)}, bf16[432,384]{1,0:T(8,128)(2,1)S(1)}, u32[]{:S(2)}, u32[]{:S(2)}) collective-permute-start(bf16[432,384]{1,0:T(8,128)(2,1)S(1)} %collective-permute-done.8), channel_id=1, source_target_pairs={{1,0},{2,1},{3,2},{4,3},{5,4},{6,5},{7,6},{8,7},{9,8},{10,9},{11,1... | collective-permute-start | bytes 995336 | tf_op jit(solution)/shard_map/ppermute | solution.py:75
  27.7 8.3 %copy-start.4 = (bf16[432,384]{1,0:T(8,128)(2,1)}, bf16[432,384]{1,0:T(8,128)(2,1)S(1)}, u32[]{:S(2)}) copy-start(bf16[432,384]{1,0:T(8,128)(2,1)S(1)} %collective-permute-done.2) | copy-start | bytes 995332
  27.7 7.8 %collective-permute-start.3 = (bf16[432,384]{1,0:T(8,128)(2,1)S(1)}, bf16[432,384]{1,0:T(8,128)(2,1)S(1)}, u32[]{:S(2)}, u32[]{:S(2)}) collective-permute-start(bf16[432,384]{1,0:T(8,128)(2,1)S(1)} %collective-permute-done.2), channel_id=1, source_target_pairs={{0,1},{1,2},{2,3},{3,4},{4,5},{5,6},{6,7},{7,8},{8,9},{9,10},{10,1... | collective-permute-start | bytes 995336 | tf_op jit(solution)/shard_map/ppermute | solution.py:73
  27.7 0.8 copy-start.2
  28.5 7.6 %collective-permute-start.10 = (bf16[432,384]{1,0:T(8,128)(2,1)S(1)}, bf16[432,384]{1,0:T(8,128)(2,1)S(1)}, u32[]{:S(2)}, u32[]{:S(2)}) collective-permute-start(bf16[432,384]{1,0:T(8,128)(2,1)S(1)} %collective-permute-done.9), channel_id=1, source_target_pairs={{1,0},{2,1},{3,2},{4,3},{5,4},{6,5},{7,6},{8,7},{9,8},{10,9},{11,1... | collective-permute-start | bytes 995336 | tf_op jit(solution)/shard_map/ppermute | solution.py:75
  35.5 28.3 %copy-start.9 = (bf16[432,384]{1,0:T(8,128)(2,1)}, bf16[432,384]{1,0:T(8,128)(2,1)S(1)}, u32[]{:S(2)}) copy-start(bf16[432,384]{1,0:T(8,128)(2,1)S(1)} %collective-permute-done.3) | copy-start | bytes 995332
  35.5 7.8 %collective-permute-start.4 = (bf16[432,384]{1,0:T(8,128)(2,1)S(1)}, bf16[432,384]{1,0:T(8,128)(2,1)S(1)}, u32[]{:S(2)}, u32[]{:S(2)}) collective-permute-start(bf16[432,384]{1,0:T(8,128)(2,1)S(1)} %collective-permute-done.3), channel_id=1, source_target_pairs={{0,1},{1,2},{2,3},{3,4},{4,5},{5,6},{6,7},{7,8},{8,9},{9,10},{10,1... | collective-permute-start | bytes 995336 | tf_op jit(solution)/shard_map/ppermute | solution.py:73
  36.1 27.8 %copy-start.5 = (bf16[432,384]{1,0:T(8,128)(2,1)}, bf16[432,384]{1,0:T(8,128)(2,1)S(1)}, u32[]{:S(2)}) copy-start(bf16[432,384]{1,0:T(8,128)(2,1)S(1)} %collective-permute-done.10) | copy-start | bytes 995332
  36.1 17.5 %collective-permute-start.11 = (bf16[432,384]{1,0:T(8,128)(2,1)S(1)}, bf16[432,384]{1,0:T(8,128)(2,1)S(1)}, u32[]{:S(2)}, u32[]{:S(2)}) collective-permute-start(bf16[432,384]{1,0:T(8,128)(2,1)S(1)} %collective-permute-done.10), channel_id=1, source_target_pairs={{1,0},{2,1},{3,2},{4,3},{5,4},{6,5},{7,6},{8,7},{9,8},{10,9},{11,1... | collective-permute-start | bytes 995336 | tf_op jit(solution)/shard_map/ppermute | solution.py:75
  43.2 20.6 %copy-start.10 = (bf16[432,384]{1,0:T(8,128)(2,1)}, bf16[432,384]{1,0:T(8,128)(2,1)S(1)}, u32[]{:S(2)}) copy-start(bf16[432,384]{1,0:T(8,128)(2,1)S(1)} %collective-permute-done.4) | copy-start | bytes 995332
  43.2 12.7 %collective-permute-start.5 = (bf16[432,384]{1,0:T(8,128)(2,1)S(1)}, bf16[432,384]{1,0:T(8,128)(2,1)S(1)}, u32[]{:S(2)}, u32[]{:S(2)}) collective-permute-start(bf16[432,384]{1,0:T(8,128)(2,1)S(1)} %collective-permute-done.4), channel_id=1, source_target_pairs={{0,1},{1,2},{2,3},{3,4},{4,5},{5,6},{6,7},{7,8},{8,9},{9,10},{10,1... | collective-permute-start | bytes 995336 | tf_op jit(solution)/shard_map/ppermute | solution.py:73
  44.8 19.3 %all-to-all-start.1 = ((f32[16,1,64]{2,1,0:T(1,128)}), f32[16,1,64]{2,1,0:T(1,128)S(1)}, u32[]{:S(2)}, u32[]{:S(2)}) async-start(f32[16,1,64]{2,1,0:T(1,128)} %broadcast_in_dim.61), calls=%async_computation.1 | async-start | bytes 16384 | tf_op jit(solution)/shard_map/all_to_all | solution.py:41
  53.5 10.3 %copy-start.7 = (bf16[432,384]{1,0:T(8,128)(2,1)}, bf16[432,384]{1,0:T(8,128)(2,1)S(1)}, u32[]{:S(2)}) copy-start(bf16[432,384]{1,0:T(8,128)(2,1)S(1)} %collective-permute-done.11) | copy-start | bytes 995332
  53.6 7.0 %collective-permute-start.12 = (bf16[432,384]{1,0:T(8,128)(2,1)S(1)}, bf16[432,384]{1,0:T(8,128)(2,1)}, u32[]{:S(2)}, u32[]{:S(2)}) collective-permute-start(bf16[432,384]{1,0:T(8,128)(2,1)S(1)} %collective-permute-done.11), channel_id=1, source_target_pairs={{1,0},{2,1},{3,2},{4,3},{5,4},{6,5},{7,6},{8,7},{9,8},{10,9},{11,1... | collective-permute-start | bytes 995336 | tf_op jit(solution)/shard_map/ppermute | solution.py:75
  55.9 10.0 %copy-start.11 = (bf16[432,384]{1,0:T(8,128)(2,1)}, bf16[432,384]{1,0:T(8,128)(2,1)S(1)}, u32[]{:S(2)}) copy-start(bf16[432,384]{1,0:T(8,128)(2,1)S(1)} %collective-permute-done.5) | copy-start | bytes 995332
  55.9 7.9 %collective-permute-start.6 = (bf16[432,384]{1,0:T(8,128)(2,1)S(1)}, bf16[432,384]{1,0:T(8,128)(2,1)}, u32[]{:S(2)}, u32[]{:S(2)}) collective-permute-start(bf16[432,384]{1,0:T(8,128)(2,1)S(1)} %collective-permute-done.5), channel_id=1, source_target_pairs={{0,1},{1,2},{2,3},{3,4},{4,5},{5,6},{6,7},{7,8},{8,9},{9,10},{10,1... | collective-permute-start | bytes 995336 | tf_op jit(solution)/shard_map/ppermute | solution.py:73
  60.6 12.6 %collective-permute-start.13 = (bf16[432,384]{1,0:T(8,128)(2,1)}, bf16[432,384]{1,0:T(8,128)(2,1)}, u32[]{:S(2)}, u32[]{:S(2)}) collective-permute-start(bf16[432,384]{1,0:T(8,128)(2,1)} %collective-permute-done.12), channel_id=1, source_target_pairs={{1,0},{2,1},{3,2},{4,3},{5,4},{6,5},{7,6},{8,7},{9,8},{10,9},{11,1... | collective-permute-start | bytes 995336 | tf_op jit(solution)/shard_map/ppermute | solution.py:75
  63.8 11.8 %collective-permute-start.7 = (bf16[432,384]{1,0:T(8,128)(2,1)}, bf16[432,384]{1,0:T(8,128)(2,1)}, u32[]{:S(2)}, u32[]{:S(2)}) collective-permute-start(bf16[432,384]{1,0:T(8,128)(2,1)} %collective-permute-done.6), channel_id=1, source_target_pairs={{0,1},{1,2},{2,3},{3,4},{4,5},{5,6},{6,7},{7,8},{8,9},{9,10},{10,1... | collective-permute-start | bytes 995336 | tf_op jit(solution)/shard_map/ppermute | solution.py:73
  65.9 43.6 %all-to-all-start = ((bf16[16,2,256,128]{3,2,1,0:T(8,128)(2,1)}), bf16[16,2,256,128]{3,2,1,0:T(8,128)(2,1)S(1)}, u32[]{:S(2)}, u32[]{:S(2)}) async-start(bf16[16,2,256,128]{3,2,1,0:T(8,128)(2,1)} %bitcast.144), calls=%async_computation | async-start | bytes 4194304 | tf_op jit(solution)/shard_map/all_to_all | solution.py:88
  73.2 15.9 %copy-start.3 = (bf16[432,384]{1,0:T(8,128)(2,1)S(1)}, bf16[432,384]{1,0:T(8,128)(2,1)}, u32[]{:S(2)}) copy-start(bf16[432,384]{1,0:T(8,128)(2,1)} %copy-done.2) | copy-start | bytes 995332
  73.2 16.7 %copy-start.6 = (bf16[432,384]{1,0:T(8,128)(2,1)S(1)}, bf16[432,384]{1,0:T(8,128)(2,1)}, u32[]{:S(2)}) copy-start(bf16[432,384]{1,0:T(8,128)(2,1)} %copy-done.5) | copy-start | bytes 995332
  73.2 17.4 %copy-start.8 = (bf16[432,384]{1,0:T(8,128)(2,1)S(1)}, bf16[432,384]{1,0:T(8,128)(2,1)}, u32[]{:S(2)}) copy-start(bf16[432,384]{1,0:T(8,128)(2,1)} %copy-done.7) | copy-start | bytes 995332
  73.2 21.6 %collective-permute-start.14 = (bf16[432,384]{1,0:T(8,128)(2,1)}, bf16[432,384]{1,0:T(8,128)(2,1)S(1)}, u32[]{:S(2)}, u32[]{:S(2)}) collective-permute-start(bf16[432,384]{1,0:T(8,128)(2,1)} %collective-permute-done.13), channel_id=1, source_target_pairs={{1,0},{2,1},{3,2},{4,3},{5,4},{6,5},{7,6},{8,7},{9,8},{10,9},{11,1... | collective-permute-start | bytes 995336 | tf_op jit(solution)/shard_map/ppermute | solution.py:75
  101.8 5.8 %copy-start.12 = (bf16[64,256]{1,0:T(8,128)(2,1)S(1)}, bf16[64,256]{1,0:T(8,128)(2,1)}, u32[]{:S(2)}) copy-start(bf16[64,256]{1,0:T(8,128)(2,1)} %param.8) | copy-start | bytes 98308
  105.3 2.3 %copy-start = (bf16[16,54,8,384]{3,2,0,1:T(8,128)(2,1)}, bf16[16,54,8,384]{3,2,0,1:T(8,128)(2,1)S(1)}, u32[]{:S(2)}) copy-start(bf16[16,54,8,384]{3,2,0,1:T(8,128)(2,1)S(1)} %copy.71) | copy-start | bytes 15925252
  111.9 9.0 %copy-start.13 = (s32[1,64]{1,0:T(1,128)S(1)}, s32[1,64]{1,0:T(1,128)}, u32[]{:S(2)}) copy-start(s32[1,64]{1,0:T(1,128)} %param.15) | copy-start | bytes 772
  113.6 27.2 %all-to-all-start.2 = ((f32[16,64,384]{2,1,0:T(8,128)}), f32[16,64,384]{2,1,0:T(8,128)}, u32[]{:S(2)}, u32[]{:S(2)}) async-start(f32[16,64,384]{2,1,0:T(8,128)} %maximum_bitcast_fusion), calls=%async_computation.2 | async-start | bytes 3145728 | tf_op jit(solution)/shard_map/all_to_all | solution.py:101
  132.1 15.7 %copy-start.1 = (bf16[256,16,256]{0,2,1:T(8,128)(2,1)S(1)}, bf16[256,16,256]{0,2,1:T(8,128)(2,1)}, u32[]{:S(2)}) copy-start(bf16[256,16,256]{0,2,1:T(8,128)(2,1)} %copy.66) | copy-start | bytes 6291460
  142.4 4.9 %collective-permute-start.15 = (bf16[64,128]{1,0:T(8,128)(2,1)S(1)}, bf16[64,128]{1,0:T(8,128)(2,1)S(1)}, u32[]{:S(2)}, u32[]{:S(2)}) collective-permute-start(bf16[64,128]{1,0:T(8,128)(2,1)S(1)} %slice.40), channel_id=1, source_target_pairs={{0,16},{16,0},{32,48},{48,32},{64,80},{80,64},{96,112},{112,96},{1... | collective-permute-start | bytes 49160 | tf_op jit(solution)/shard_map/ppermute | solution.py:105
